TPU v7x, 32 devices: a whole 2x2x4 slice. The times are simulated.
32 devices in a mesh: mkt: 8 (over z, y), draw: 4 (over x, core).
Axes of the slice: x: 2, y: 2, z: 4, core: 2. Of those that a mesh axis runs over, the one named last changes fastest.
Arguments:
- x_char: float32 [384, 56, 8], P('mkt'), may hold values from -2.5 to 2.5
- nu_draws: float32 [384, 8, 2048], P('mkt', None, 'draw'), may hold values from -3 to 3
- coef_sigma: float32 [8], replicated, may hold values from 0.3 to 1.2
- log_share: float32 [384, 56], P('mkt'), may hold values from -7 to -4.5
- counts: int32 [384], P('mkt'), may hold values from 28 to 56
Outputs:
- mean_util: float32 [384, 56], P('mkt')
- jacobian: float32 [384, 56, 56], P(('mkt', 'draw'))
- sup_norms: float32 [3], replicated
Inputs may be any that keep to these rules, and one draw needn't show every extreme that they name: Products 0 to counts - 1 of a market are valid; the other slots are padding.
All inputs are finite; a program needn't handle non-finite values. Where the computation divides by a largest or mean magnitude, that divisor is 1e-20 or more.
Results may differ from a plain program's by a relative error of at most 0.00013.
Values sent between devices are 32-bit elements; how exact they have to be, the bound alone decides.
A program may use at most 64 MiB of HBM per device.

v0:
```python
import jax
import jax.numpy as jnp
from jax import lax
from jax.sharding import PartitionSpec as P

ITERS = 3


step_cap = 0.25
epsilon = 1e-06


def market_terms(mean_util, scaled, nu_draws, usable, inverse, with_products):
    tastes = jnp.einsum("mjk,mkr->mjr", scaled, nu_draws, precision=lax.Precision.HIGHEST)
    raised = jnp.where(usable[:, :, None], jnp.exp(mean_util[:, :, None] + tastes), 0.0)
    chance = raised / (1.0 + jnp.sum(raised, axis=1, keepdims=True))
    shares = jnp.sum(chance, axis=2) * inverse
    if with_products:
        cross_sums = (
            jnp.einsum("mjr,mlr->mjl", chance, chance, precision=lax.Precision.HIGHEST) * inverse
        )
        return (shares, cross_sums)
    return shares


def evaluate(mean_util, scaled, nu_draws, usable, inverse, with_products):
    groups = mean_util.shape[0] // 8
    folded = (
        mean_util.reshape(groups, 8, mean_util.shape[1]),
        scaled.reshape(groups, 8, scaled.shape[1], scaled.shape[2]),
        nu_draws.reshape(groups, 8, nu_draws.shape[1], nu_draws.shape[2]),
        usable.reshape(groups, 8, usable.shape[1]),
    )

    def per_group(items):
        return market_terms(items[0], items[1], items[2], items[3], inverse, with_products)

    def unfold(member):
        return member.reshape((groups * 8,) + member.shape[2:])

    return jax.tree.map(unfold, lax.map(per_group, folded))


def contraction(log_share, shares, usable):
    return jnp.where(usable, log_share - jnp.log(jnp.where(usable, shares, 1.0)), 0.0)


def step_size(largest):
    return jnp.minimum(1.0, step_cap / (largest + epsilon))


def jacobian_rows(shares, cross_sums, usable):
    slots = shares.shape[1]
    divisor = jnp.where(usable, shares, 1.0)
    identity = jnp.eye(slots, dtype=jnp.float32)
    paired = usable[:, :, None] & usable[:, None, :]
    return jnp.where(paired, identity[None, :, :] - cross_sums / divisor[:, :, None], 0.0)


def whole_sweeps(
    mean_util, scaled, nu_draws, usable, log_share, inverse, total_fn, peak_fn, final_fn
):
    norms_list = []
    for sweep in range(ITERS):
        partial_value = evaluate(mean_util, scaled, nu_draws, usable, inverse, False)
        shares = total_fn(partial_value)
        change = contraction(log_share, shares, usable)
        largest = peak_fn(jnp.max(jnp.abs(change)))
        mean_util = mean_util + step_size(largest) * change
        norms_list.append(largest)
    partial_value, cross_part = evaluate(mean_util, scaled, nu_draws, usable, inverse, True)
    shares, summed = final_fn(partial_value, cross_part)
    return (mean_util, shares, summed, norms_list)


def shards(x_char, nu_draws, coef_sigma, log_share, counts):
    slots = log_share.shape[1]
    markets = log_share.shape[0]
    draw_count = lax.axis_size("draw")
    inverse = 1.0 / (nu_draws.shape[2] * draw_count)
    usable = jnp.arange(slots, dtype=jnp.int32)[None, :] < counts[:, None]
    scaled = x_char * coef_sigma[None, None, :]
    inside = jnp.sum(jnp.where(usable, jnp.exp(log_share), 0.0), axis=1)
    mean_util = jnp.where(usable, log_share - jnp.log(1.0 - inside)[:, None], 0.0)
    own_rows = markets // draw_count
    first_row = lax.axis_index("draw") * own_rows
    usable_own = lax.dynamic_slice_in_dim(usable, first_row, own_rows, 0)

    def total_market(partial_value):
        return lax.psum(partial_value, "draw")

    def peak_market(local):
        return lax.pmax(local, "mkt")

    def final_market(partial_value, cross_part):
        return lax.psum((partial_value, cross_part), "draw")

    mean_util, shares, cross_sums, norms_list = whole_sweeps(
        mean_util,
        scaled,
        nu_draws,
        usable,
        log_share,
        inverse,
        total_market,
        peak_market,
        final_market,
    )
    jacobian = jacobian_rows(
        lax.dynamic_slice_in_dim(shares, first_row, own_rows, 0),
        lax.dynamic_slice_in_dim(cross_sums, first_row, own_rows, 0),
        usable_own,
    )
    return (mean_util, jacobian, jnp.stack(norms_list))


def solution(mesh):
    return jax.shard_map(
        shards,
        mesh=mesh,
        in_specs=(P("mkt", None, None), P("mkt", None, "draw"), P(), P("mkt", None), P("mkt")),
        out_specs=(P("mkt", None), P(("mkt", "draw"), None, None), P()),
        check_vma=False,
    )
```

profile of v0, /device:TPU:0, one launch (start us, length us, event | category | flops | bytes accessed | tf_op | source)
XLA Modules:
  0.0 216.6 jit_solution(17408170341341090726)
XLA Ops:
  10.8 13.2 %while.42 = (s32[]{:T(128)}, f32[6,8,56]{2,1,0:T(8,128)S(1)}, pred[6,8,56]{2,1,0:T(8,128)(4,1)S(1)}, f32[6,8,56]{2,1,0:T(8,128)S(1)}, f32[6,8,56,8]{2,3,1,0:T(8,128)S(1)}, /*index=5*/f32[6,8,8,512]{3,2,1,0:T(8,128)}, s32[]{:T(128)}) while((s32[]{:T(128)}, f32[6,8,56]{2,1,0:T(8,128)S(1)}, pred[6,8,56]{2,1,0:T(8,128)(4,1)S(1)}, ...), condition=%wide.region_4.5_spmd, body=%wide.region_1.4_spmd.sunk | while | flops 23166976 | bytes 2085081 | solution.py:41
  10.9 2.0 fusion.44
  13.1 2.0 fusion.44
  15.3 2.0 fusion.44
  17.5 2.0 fusion.44
  24.0 12.9 %psum.35 = f32[48,56]{1,0:T(8,128)S(1)} all-reduce(f32[48,56]{1,0:T(8,128)S(1)} %bitcast.133), channel_id=1, replica_groups=mesh['mkt'=8,'draw'=4] {'draw'}, use_global_device_ids=true, to_apply=%region_5.6 | all-reduce | flops 2688 | bytes 21504 | tf_op jit(solution)/shard_map/psum | solution.py:90
  37.6 22.3 %pmax.21 = f32[]{:T(128)} all-reduce(f32[]{:T(128)} %abs_reduce_fusion.2), channel_id=1, replica_groups=mesh['mkt'=8,'draw'=4] {'mkt'}, use_global_device_ids=true, to_apply=%region_7.8 | all-reduce | flops 1 | bytes 8 | tf_op jit(solution)/shard_map/pmax | solution.py:93
  60.7 13.2 %while.43 = (s32[]{:T(128)}, f32[6,8,56]{2,1,0:T(8,128)S(1)}, pred[6,8,56]{2,1,0:T(8,128)(4,1)S(1)}, f32[6,8,56]{2,1,0:T(8,128)S(1)}, f32[6,8,56,8]{2,3,1,0:T(8,128)S(1)}, /*index=5*/f32[6,8,8,512]{3,2,1,0:T(8,128)}, s32[]{:T(128)}) while((s32[]{:T(128)}, f32[6,8,56]{2,1,0:T(8,128)S(1)}, pred[6,8,56]{2,1,0:T(8,128)(4,1)S(1)}, ...), condition=%wide.region_11.12_spmd, body=%wide.region_8.11_spmd.sunk | while | flops 23166976 | bytes 2085081 | solution.py:41
  60.7 2.0 fusion.45
  62.9 2.0 fusion.45
  65.1 2.0 fusion.45
  67.3 2.0 fusion.45
  69.5 2.0 fusion.45
  71.7 2.0 fusion.45
  73.9 10.3 %psum.36 = f32[48,56]{1,0:T(8,128)S(1)} all-reduce(f32[48,56]{1,0:T(8,128)S(1)} %bitcast.134), channel_id=1, replica_groups=mesh['mkt'=8,'draw'=4] {'draw'}, use_global_device_ids=true, to_apply=%region_12.13 | all-reduce | flops 2688 | bytes 21504 | tf_op jit(solution)/shard_map/psum | solution.py:90
  84.9 17.8 %pmax.22 = f32[]{:T(128)} all-reduce(f32[]{:T(128)} %get-tuple-element.192), channel_id=1, replica_groups=mesh['mkt'=8,'draw'=4] {'mkt'}, use_global_device_ids=true, to_apply=%region_14.15 | all-reduce | flops 1 | bytes 8 | tf_op jit(solution)/shard_map/pmax | solution.py:93
  103.4 13.2 %while.44 = (s32[]{:T(128)}, f32[6,8,56]{2,1,0:T(8,128)S(1)}, pred[6,8,56]{2,1,0:T(8,128)(4,1)S(1)}, f32[6,8,56]{2,1,0:T(8,128)S(1)}, f32[6,8,56,8]{2,3,1,0:T(8,128)S(1)}, /*index=5*/f32[6,8,8,512]{3,2,1,0:T(8,128)}, s32[]{:T(128)}) while((s32[]{:T(128)}, f32[6,8,56]{2,1,0:T(8,128)S(1)}, pred[6,8,56]{2,1,0:T(8,128)(4,1)S(1)}, ...), condition=%wide.region_18.19_spmd, body=%wide.region_15.18_spmd.sunk | while | flops 23166976 | bytes 2085081 | solution.py:41
  116.6 10.3 %psum.37 = f32[48,56]{1,0:T(8,128)S(1)} all-reduce(f32[48,56]{1,0:T(8,128)S(1)} %bitcast.135), channel_id=1, replica_groups=mesh['mkt'=8,'draw'=4] {'draw'}, use_global_device_ids=true, to_apply=%region_19.20 | all-reduce | flops 2688 | bytes 21504 | tf_op jit(solution)/shard_map/psum | solution.py:90
  127.6 19.8 %pmax.23 = f32[]{:T(128)} all-reduce(f32[]{:T(128)} %abs_reduce_fusion), channel_id=1, replica_groups=mesh['mkt'=8,'draw'=4] {'mkt'}, use_global_device_ids=true, to_apply=%region_21.22 | all-reduce | flops 1 | bytes 8 | tf_op jit(solution)/shard_map/pmax | solution.py:93
  148.0 23.3 %while.45 = (s32[]{:T(128)}, f32[6,8,56]{2,1,0:T(8,128)S(1)}, f32[6,8,56,56]{3,2,1,0:T(8,128)}, pred[6,8,56]{2,1,0:T(8,128)(4,1)S(1)}, f32[6,8,56]{2,1,0:T(8,128...) while((s32[]{:T(128)}, f32[6,8,56]{2,1,0:T(8,128)S(1)}, ...), condition=%wide.region_25.26_spmd, body=%wide.region_22.25_spmd.sunk | while | flops 177562112 | bytes 3248865 | solution.py:41
  167.5 2.0 fusion.47
  171.4 11.7 %psum.39 = f32[48,56]{1,0:T(8,128)S(1)} all-reduce(f32[48,56]{1,0:T(8,128)S(1)} %bitcast.132), channel_id=1, replica_groups=mesh['mkt'=8,'draw'=4] {'draw'}, use_global_device_ids=true, to_apply=%region_27.28 | all-reduce | flops 2688 | bytes 21504 | tf_op jit(solution)/shard_map/psum | solution.py:96
  183.1 2.5 %pad_maximum_fusion = f32[3]{0:T(128)} fusion(f32[1]{0:T(128)} %bitcast.34, f32[1]{0:T(128)} %bitcast.33, f32[1]{0:T(128)} %bitcast.32), kind=kLoop, calls=%fused_computation.77 | loop fusion | flops 6 | bytes 24 | tf_op jit(solution)/shard_map/stack | solution.py:114
  185.6 22.2 %all-reduce.2.cloned.1.call-done = f32[48,56,56]{2,1,0:T(8,128)} async-done(((f32[48,56,56]{2,1,0:T(8,128)}), f32[48,56,56]{2,1,0:T(8,128)}) %all-reduce.2.cloned.1.call-update) | async-done | bytes 602128 | tf_op jit(solution)/shard_map/psum | solution.py:96
  (169 shorter events, 47.8 us)
Async XLA Ops:
  7.2 200.7 %all-reduce.2.cloned.1.call-start = ((), (), s32[]{:S(2)}) async-start(), calls=%async_computation | async-start | bytes 2752512 | tf_op jit(solution)/shard_map/psum | solution.py:96
  10.8 26.1 %copy-start = (f32[48,56]{1,0:T(8,128)S(1)}, f32[48,56]{1,0:T(8,128)}, u32[]{:S(2)}) copy-start(f32[48,56]{1,0:T(8,128)} %param.16) | copy-start | bytes 32260
  10.8 26.1 %copy-start.2 = (s32[48]{0:T(128)S(1)}, s32[48]{0:T(128)}, u32[]{:S(2)}) copy-start(s32[48]{0:T(128)} %param.17) | copy-start | bytes 580
  171.3 38.4 %copy-start.1 = (f32[6,8,56]{2,1,0:T(8,128)}, f32[6,8,56]{2,1,0:T(8,128)S(1)}, u32[]{:S(2)}) copy-start(f32[6,8,56]{2,1,0:T(8,128)S(1)} %get-tuple-element.473) | copy-start | bytes 32260
Sparse Core Ops, SparseCore 0:
  171.5 36.2 all-reduce.1
where the time goes:
time: 218 us; the launch traced here: 217 us
  blocking collectives  105 us (48%)
  matrix products  57.1 us (26%)
  waiting for transfers between devices  22.2 us (10%)
  between operations  16.2 us (7%)
  other arithmetic  13.4 us (6%)
    pmax x3, blocking collectives, peak_market(): return lax.pmax(local, 'mkt')  59.9 us
    dot_general x24, matrix products, market_terms(): jnp.einsum('mjk,mkr->mjr', scaled, nu_draws, precision=lax.Precision.HIGH...  47 us
    psum x3, blocking collectives, total_market(): return lax.psum(partial_value, 'draw')  33.4 us
    psum x1, waiting for transfers between devices, final_market(): return lax.psum((partial_value, cross_part), 'draw')  22.2 us
    psum x1, blocking collectives, final_market(): return lax.psum((partial_value, cross_part), 'draw')  11.7 us
    dot_general x6, matrix products, market_terms(): jnp.einsum('mjr,mlr->mjl', chance, chance, precision=lax.Precision.HIGHEST)  10.1 us
  transfers between devices with their start and end apart: 1, of which 1 were waited for; matrix products, arithmetic and copies ran while one was open for 1% of the time, Pallas kernels for 0%

commit v1 on v0

v1 whole, which is shorter than its diff:
```python
import functools
import math

import jax
import jax.numpy as jnp
from jax import lax
from jax.experimental import pallas as pl
from jax.experimental.pallas import tpu as pltpu
from jax.sharding import PartitionSpec as P

ITERS = 3
LANES = 128
MESH = pl.DeviceIdType.MESH

step_cap = 0.25
epsilon = 1e-06


def divisor_up_to(count, most):
    return max(size for size in range(1, most + 1) if count % size == 0)


def rounded(value):
    return value.astype(jnp.bfloat16).astype(jnp.float32)


def split3(value):
    first = rounded(value)
    second = rounded(value - first)
    return first, second, (value - first) - second


def kernel(
    draws,
    chips,
    inverse,
    sigma_ref,
    counts_ref,
    counts_row_ref,
    log_share_ref,
    x_ref,
    nu_ref,
    mean_out,
    jac_out,
    norms_out,
    held,
    square,
    part_slots,
    peak_slots,
    cross_send,
    cross_slots,
    part_send_sem,
    part_recv_sem,
    peak_send_sem,
    peak_recv_sem,
    cross_send_sem,
    cross_recv_sem,
):
    markets, coefs, slots = x_ref.shape
    own = markets // draws
    half = LANES // 2 if slots + 8 <= LANES // 2 else LANES
    pack = LANES // half
    group = divisor_up_to(markets, 8)
    my_draw = lax.axis_index("draw")
    my_mkt = lax.axis_index("mkt")

    barrier = pltpu.get_barrier_semaphore()
    for k in range(1, draws):
        pl.semaphore_signal(
            barrier, inc=1, device_id={"draw": lax.rem(my_draw + k, draws)}, device_id_type=MESH
        )
    for k in range(1, chips):
        pl.semaphore_signal(
            barrier, inc=1, device_id={"mkt": lax.rem(my_mkt + k, chips)}, device_id_type=MESH
        )

    lane = lax.broadcasted_iota(jnp.int32, (slots, LANES), 1)
    row = lax.broadcasted_iota(jnp.int32, (slots, LANES), 0)

    square[...] = jnp.zeros_like(square)
    square[0:markets, 0:slots] = log_share_ref[...]
    log_share = square[...].T[0:slots, :]
    square[0:1, 0:markets] = counts_row_ref[...].astype(jnp.float32)
    counts = square[0:1, :]
    usable = (row.astype(jnp.float32) < counts) & (lane < markets)
    inside = jnp.sum(jnp.where(usable, jnp.exp(log_share), 0.0), axis=0, keepdims=True)
    mean = jnp.where(usable, log_share - jnp.log(1.0 - inside), 0.0)

    coef_row = lax.broadcasted_iota(jnp.int32, (coefs, slots), 0)
    sigma = jnp.zeros((coefs, slots), jnp.float32)
    for k in range(coefs):
        sigma = jnp.where(coef_row == k, sigma_ref[k], sigma)

    def raised_tastes(m):
        s1, s2, s3 = split3(x_ref[m] * sigma * math.log2(math.e))
        n1, n2, n3 = split3(nu_ref[m])
        left = jnp.concatenate([s1, s1, s2, s2, s1, s3], axis=0).astype(jnp.bfloat16)
        right = jnp.concatenate([n1, n2, n1, n2, n3, n1], axis=0).astype(jnp.bfloat16)
        tastes = lax.dot_general(
            left, right, (((0,), (0,)), ((), ())), preferred_element_type=jnp.float32
        )
        return jnp.exp2(tastes)

    def sweep(weights, first):
        def body(g, total):
            base = g * group
            local = pltpu.roll(weights, lax.rem(LANES - base, LANES), 1)
            part = jnp.zeros((slots, LANES), jnp.float32)
            for i in range(group):
                if first:
                    e = raised_tastes(base + i)
                    held[base + i] = e
                else:
                    e = held[base + i]
                denominator = 1.0 + jnp.sum(local[:, i : i + 1] * e, axis=0, keepdims=True)
                column = jnp.sum(e * (1.0 / denominator), axis=1, keepdims=True)
                part = jnp.where(lane == i, column, part)
            return total + pltpu.roll(part, base, 1)

        return lax.fori_loop(0, markets // group, body, jnp.zeros((slots, LANES), jnp.float32))

    def part_copy(it, k):
        return pltpu.make_async_remote_copy(
            src_ref=part_slots.at[it, my_draw],
            dst_ref=part_slots.at[it, my_draw],
            send_sem=part_send_sem.at[it, k - 1],
            recv_sem=part_recv_sem.at[it, k - 1],
            device_id={"draw": lax.rem(my_draw + k, draws)},
            device_id_type=MESH,
        )

    def peak_copy(it, k):
        return pltpu.make_async_remote_copy(
            src_ref=peak_slots.at[it, 0],
            dst_ref=peak_slots.at[it, k],
            send_sem=peak_send_sem.at[it, k - 1],
            recv_sem=peak_recv_sem.at[it, k - 1],
            device_id={"mkt": lax.rem(my_mkt + k, chips)},
            device_id_type=MESH,
        )

    for it in range(ITERS):
        weights = jnp.where(usable, jnp.exp(mean), 0.0)
        partial_value = sweep(weights, it == 0)
        part_slots[it, my_draw] = partial_value
        if it == 0:
            pl.semaphore_wait(barrier, draws - 1 + chips - 1)
        for k in range(1, draws):
            part_copy(it, k).start()
        for k in range(1, draws):
            part_copy(it, k).wait()
        total = part_slots[it, 0]
        for d in range(1, draws):
            total = total + part_slots[it, d]
        shares = weights * total * inverse
        change = jnp.where(usable, log_share - jnp.log(jnp.where(usable, shares, 1.0)), 0.0)
        peak = jnp.max(jnp.abs(change), axis=0, keepdims=True)
        peak = jnp.max(peak, axis=1, keepdims=True)
        peak_slots[it, 0] = jnp.broadcast_to(peak, (8, LANES))
        for k in range(1, chips):
            peak_copy(it, k).start()
        for k in range(1, chips):
            peak_copy(it, k).wait()
        largest = peak_slots[it, 0]
        for k in range(1, chips):
            largest = jnp.maximum(largest, peak_slots[it, k])
        norms_out[it] = largest[0, 0]
        largest = largest[0:1, :]
        mean = mean + jnp.minimum(1.0, step_cap / (largest + epsilon)) * change

    weights = jnp.where(usable, jnp.exp(mean), 0.0)
    ones = jnp.ones((8, nu_ref.shape[2]), jnp.float32)
    doubled = jnp.where(
        lax.broadcasted_iota(jnp.int32, (slots, slots + 8), 1) < slots, 2.0, 1.0
    )

    def cross_copy(k):
        return pltpu.make_async_remote_copy(
            src_ref=cross_send.at[k - 1],
            dst_ref=cross_slots.at[k - 1],
            send_sem=cross_send_sem.at[k - 1],
            recv_sem=cross_recv_sem.at[k - 1],
            device_id={"draw": lax.rem(my_draw + k, draws)},
            device_id_type=MESH,
        )

    def last_sweep(k, carry):
        base = lax.rem(my_draw + k, draws) * own
        local = pltpu.roll(weights, lax.rem(LANES - base, LANES), 1)
        for i in range(own):
            e = held[base + i]
            raised = local[:, i : i + 1] * e
            denominator = 1.0 + jnp.sum(raised, axis=0, keepdims=True)
            chance = raised * (1.0 / denominator)
            both = jnp.concatenate([chance, chance - rounded(chance)], axis=0)
            right = jnp.concatenate([chance, ones], axis=0).astype(jnp.bfloat16)
            products = lax.dot_general(
                both.astype(jnp.bfloat16),
                right,
                (((1,), (1,)), ((), ())),
                preferred_element_type=jnp.float32,
            )
            merged = products[0:slots] + products[slots:] * doubled
            at = (i % pack) * half
            cross_send[k - 1, i // pack, :, at : at + slots + 8] = merged

        @pl.when(k < draws)
        def _():
            cross_copy(k).start()

        return carry

    lax.fori_loop(1, draws + 1, last_sweep, 0)

    square[0:slots, :] = mean
    mean_out[...] = square[...].T[0:markets, 0:slots]

    for k in range(1, draws):
        cross_copy(k).wait()

    eye = (row == lane)[:, 0:slots]
    for pair in range(cross_send.shape[1]):
        total = cross_send[draws - 1, pair]
        for k in range(1, draws):
            total = total + cross_slots[k - 1, pair]
        for i in range(pack):
            if pair * pack + i >= own:
                continue
            wide = total if i == 0 else pltpu.roll(total, LANES - i * half, 1)
            square[0:slots, :] = wide
            turned = square[...].T[0:slots, 0:slots]
            cross = 0.5 * (wide[:, 0:slots] + turned)
            count = counts_ref[my_draw * own + pair * pack + i]
            here = row < count
            divisor = jnp.where(here, wide, 1.0)[:, slots : slots + 1]
            jac_out[pair * pack + i] = jnp.where(
                (here & (lane < count))[:, 0:slots],
                jnp.where(eye, 1.0, 0.0) - cross / divisor,
                0.0,
            )


def shards(x_char, nu_draws, coef_sigma, log_share, counts):
    markets, slots, coefs = x_char.shape
    consumers = nu_draws.shape[2]
    draws, chips = lax.axis_size("draw"), lax.axis_size("mkt")
    own = markets // draws
    half = LANES // 2 if slots + 8 <= LANES // 2 else LANES
    blocks = -(-own // (LANES // half))
    vmem = pl.BlockSpec(memory_space=pltpu.VMEM)
    smem = pl.BlockSpec(memory_space=pltpu.SMEM)
    f32 = jnp.float32
    return pl.pallas_call(
        functools.partial(kernel, draws, chips, 1.0 / (consumers * draws)),
        out_shape=(
            jax.ShapeDtypeStruct((markets, slots), f32),
            jax.ShapeDtypeStruct((own, slots, slots), f32),
            jax.ShapeDtypeStruct((ITERS,), f32),
        ),
        in_specs=[smem, smem, vmem, vmem, vmem, vmem],
        out_specs=(vmem, vmem, smem),
        scratch_shapes=[
            pltpu.VMEM((markets, slots, consumers), f32),
            pltpu.VMEM((LANES, LANES), f32),
            pltpu.VMEM((ITERS, draws, slots, LANES), f32),
            pltpu.VMEM((ITERS, chips, 8, LANES), f32),
            pltpu.VMEM((draws, blocks, slots, LANES), f32),
            pltpu.VMEM((draws, blocks, slots, LANES), f32),
            pltpu.SemaphoreType.DMA((ITERS, draws)),
            pltpu.SemaphoreType.DMA((ITERS, draws)),
            pltpu.SemaphoreType.DMA((ITERS, chips)),
            pltpu.SemaphoreType.DMA((ITERS, chips)),
            pltpu.SemaphoreType.DMA((draws,)),
            pltpu.SemaphoreType.DMA((draws,)),
        ],
        compiler_params=pltpu.CompilerParams(
            collective_id=0, has_side_effects=True, vmem_limit_bytes=48 * 1024 * 1024
        ),
        name="contraction",
    )(
        coef_sigma,
        counts,
        counts[None, :],
        log_share,
        jnp.swapaxes(x_char, 1, 2),
        nu_draws,
    )


def solution(mesh):
    return jax.shard_map(
        shards,
        mesh=mesh,
        in_specs=(P("mkt", None, None), P("mkt", None, "draw"), P(), P("mkt", None), P("mkt")),
        out_specs=(P("mkt", None), P(("mkt", "draw"), None, None), P()),
        check_vma=False,
    )
```

time: 218 us -> 53.7 us (0.25)
  blocking collectives: 105 us -> 0 us
  matrix products: 57.1 us -> 0 us
  Pallas kernels: 0 us -> 47.2 us
  waiting for transfers between devices: 22.2 us -> 0 us
  between operations: 16.2 us -> 0.66 us
  other arithmetic: 13.4 us -> 0 us
  local copies, waits for them, and re-layouts: 1.2 us -> 5.3 us
    pmax x3 -> x0, blocking collectives: 59.9 us -> none  [peak_market(): return lax.pmax(local, 'mkt')]
    dot_general x30 -> x0, matrix products: 57.1 us -> none  [the longest x24 47 us: market_terms(): jnp.einsum('mjk,mkr->mjr', scaled, nu_draws, precision=lax.Precision.HIGH...]
    pallas_call x0 -> x1, Pallas kernels: none -> 47.2 us  [shards(): pl.pallas_call(functools.partial(kernel, draws, chips, 1.0 / (consumers *...]
    psum x4 -> x0, blocking collectives: 45.1 us -> none  [the longest x3 33.4 us: total_market(): return lax.psum(partial_value, 'draw')]
    psum x1 -> x0, waiting for transfers between devices: 22.2 us -> none  [final_market(): return lax.psum((partial_value, cross_part), 'draw')]
    unnamed x6 -> x13, local copies, waits for them, and re-layouts: 0.02 us -> 5.3 us
    reduce_sum x25 -> x0, other arithmetic: 4.46 us -> none  [the longest x24 3.54 us: market_terms(): shares = jnp.sum(chance, axis=2) * inverse]
    another operation x1 -> x0, other arithmetic: 2.48 us -> none  [shards(): return (mean_util, jacobian, jnp.stack(norms_list))]
  transfers between devices with their start and end apart: 1 -> 0, of which waited for: 1 -> 0; matrix products, arithmetic and copies ran while one was open for 1% -> 0% of each run, Pallas kernels for 0% -> 0%
where the time goes in v1:
time: 53.7 us; the launch traced here: 53.1 us
  Pallas kernels  47.2 us (88%)
  local copies, waits for them, and re-layouts  5.3 us (10%)
  between operations  0.66 us (1%)
    pallas_call x1, Pallas kernels, shards(): pl.pallas_call(functools.partial(kernel, draws, chips, 1.0 / (consumers *...  47.2 us
    unnamed x13, local copies, waits for them, and re-layouts  5.3 us

profile of v1, /device:TPU:0, one launch (start us, length us, event | category | flops | bytes accessed | tf_op | source)
XLA Modules:
  0.0 53.1 jit_solution(9830893668320656265)
XLA Ops:
  0.6 0.0 copy-start.3
  0.6 0.0 copy-start.4
  0.7 0.6 %copy-done.3 = s32[48]{0:T(128)S(1)} copy-done((s32[48]{0:T(128)S(1)}, s32[48]{0:T(128)}, u32[]{:S(2)}) %copy-start.3) | copy-done | bytes 216
  1.3 0.0 copy-done.4
  1.3 0.0 copy-start
  1.3 1.1 %copy-done = f32[48,8,512]{2,1,0:T(8,128)S(1)} copy-done((f32[48,8,512]{2,1,0:T(8,128)S(1)}, f32[48,8,512]{2,1,0:T(8,128)}, u32[]{:S(2)}) %copy-start) | copy-done | bytes 786456
  2.4 0.0 copy-start.1
  2.4 0.9 %copy-done.1 = f32[48,56,8]{1,2,0:T(8,128)S(1)} copy-done((f32[48,56,8]{1,2,0:T(8,128)S(1)}, f32[48,56,8]{1,2,0:T(8,128)}, u32[]{:S(2)}) %copy-start.1) | copy-done | bytes 86040
  3.4 0.0 copy-start.2
  3.4 0.7 %copy-done.2 = f32[48,56]{1,0:T(8,128)S(1)} copy-done((f32[48,56]{1,0:T(8,128)S(1)}, f32[48,56]{1,0:T(8,128)}, u32[]{:S(2)}) %copy-start.2) | copy-done | bytes 10776
  4.1 47.2 %contraction.1 = (f32[48,56]{1,0:T(8,128)S(1)}, f32[12,56,56]{2,1,0:T(8,128)S(1)}, f32[3]{0:T(128)S(1)}) custom-call(f32[8]{0:T(128)S(1)} %copy-done.4, s32[48]{0:T(128)S(1)} %copy-done.3, s32[1,48]{1,0:T(1,128)S(1)} %bitcast.3, f32[48,56]{1,0:T(8,128)S(1)} %copy-done.2, f32[48,8,56]{2,1,0:T(8,128)S(1)} %bitcast.2, f32[48,8,512]{2,1,0:T(8,128)S(1)} %copy-done), custom_call_target="tpu_custom_call" | custom-call | tf_op jit(solution)/shard_map/contraction/pallas_call | solution.py:253
  51.3 0.6 %copy.11 = f32[48,56]{1,0:T(8,128)} copy(f32[48,56]{1,0:T(8,128)S(1)} %get-tuple-element.6) | data formatting | bytes 21504
  51.9 0.7 %copy.12 = f32[12,56,56]{2,1,0:T(8,128)} copy(f32[12,56,56]{2,1,0:T(8,128)S(1)} %get-tuple-element.7) | data formatting | bytes 301056
  52.6 0.5 copy.13
Async XLA Ops:
  0.6 0.7 %copy-start.3 = (s32[48]{0:T(128)S(1)}, s32[48]{0:T(128)}, u32[]{:S(2)}) copy-start(s32[48]{0:T(128)} %counts_ref.1) | copy-start | bytes 580
  0.6 0.7 %copy-start.4 = (f32[8]{0:T(128)S(1)}, f32[8]{0:T(128)}, u32[]{:S(2)}) copy-start(f32[8]{0:T(128)} %sigma_ref.1) | copy-start | bytes 100
  1.3 1.1 %copy-start = (f32[48,8,512]{2,1,0:T(8,128)S(1)}, f32[48,8,512]{2,1,0:T(8,128)}, u32[]{:S(2)}) copy-start(f32[48,8,512]{2,1,0:T(8,128)} %nu_ref.1) | copy-start | bytes 2359300
  2.4 0.9 %copy-start.1 = (f32[48,56,8]{1,2,0:T(8,128)S(1)}, f32[48,56,8]{1,2,0:T(8,128)}, u32[]{:S(2)}) copy-start(f32[48,56,8]{1,2,0:T(8,128)} %param.5) | copy-start | bytes 258052
  3.4 0.7 %copy-start.2 = (f32[48,56]{1,0:T(8,128)S(1)}, f32[48,56]{1,0:T(8,128)}, u32[]{:S(2)}) copy-start(f32[48,56]{1,0:T(8,128)} %log_share_ref.1) | copy-start | bytes 32260

commit v2 on v1

--- a/solution.py
+++ b/solution.py
@@ -10,6 +10,8 @@
 
 ITERS = 3
 LANES = 128
+GROUP = 16
+VMEM_LIMIT = 66_500_000
 MESH = pl.DeviceIdType.MESH
 
 step_cap = 0.25
@@ -24,26 +26,32 @@
     return value.astype(jnp.bfloat16).astype(jnp.float32)
 
 
-def split3(value):
+def split2(value):
     first = rounded(value)
-    second = rounded(value - first)
-    return first, second, (value - first) - second
+    return first, value - first
 
 
 def kernel(
     draws,
     chips,
     inverse,
+    sigma_hbm,
+    counts_hbm,
+    counts_row_hbm,
+    log_share_hbm,
+    x_hbm,
+    nu_hbm,
+    mean_out,
+    jac_out,
+    norms_out,
     sigma_ref,
     counts_ref,
     counts_row_ref,
     log_share_ref,
     x_ref,
     nu_ref,
-    mean_out,
-    jac_out,
-    norms_out,
     held,
+    inverse_ref,
     square,
     part_slots,
     peak_slots,
@@ -55,14 +63,39 @@
     peak_recv_sem,
     cross_send_sem,
     cross_recv_sem,
+    load_sem,
+    nu_sem,
 ):
     markets, coefs, slots = x_ref.shape
     own = markets // draws
     half = LANES // 2 if slots + 8 <= LANES // 2 else LANES
     pack = LANES // half
-    group = divisor_up_to(markets, 8)
+    group = divisor_up_to(markets, GROUP)
+    folds = part_slots.shape[2]
     my_draw = lax.axis_index("draw")
     my_mkt = lax.axis_index("mkt")
+
+    loads = [
+        pltpu.make_async_copy(source, target, load_sem.at[n])
+        for n, (source, target) in enumerate(
+            (
+                (counts_row_hbm, counts_row_ref),
+                (log_share_hbm, log_share_ref),
+                (sigma_hbm, sigma_ref),
+                (counts_hbm, counts_ref),
+                (x_hbm, x_ref),
+            )
+        )
+    ]
+
+    def nu_load(g):
+        span = pl.ds(g * group, group)
+        return pltpu.make_async_copy(nu_hbm.at[span], nu_ref.at[span], nu_sem.at[g])
+
+    for load in loads:
+        load.start()
+    for g in range(markets // group):
+        nu_load(g).start()
 
     barrier = pltpu.get_barrier_semaphore()
     for k in range(1, draws):
@@ -78,6 +111,8 @@
     row = lax.broadcasted_iota(jnp.int32, (slots, LANES), 0)
 
     square[...] = jnp.zeros_like(square)
+    for load in loads:
+        load.wait()
     square[0:markets, 0:slots] = log_share_ref[...]
     log_share = square[...].T[0:slots, :]
     square[0:1, 0:markets] = counts_row_ref[...].astype(jnp.float32)
@@ -89,35 +124,65 @@
     coef_row = lax.broadcasted_iota(jnp.int32, (coefs, slots), 0)
     sigma = jnp.zeros((coefs, slots), jnp.float32)
     for k in range(coefs):
-        sigma = jnp.where(coef_row == k, sigma_ref[k], sigma)
+        sigma = jnp.where(coef_row == k, sigma_ref[k] * math.log2(math.e), sigma)
 
     def raised_tastes(m):
-        s1, s2, s3 = split3(x_ref[m] * sigma * math.log2(math.e))
-        n1, n2, n3 = split3(nu_ref[m])
-        left = jnp.concatenate([s1, s1, s2, s2, s1, s3], axis=0).astype(jnp.bfloat16)
-        right = jnp.concatenate([n1, n2, n1, n2, n3, n1], axis=0).astype(jnp.bfloat16)
+        s1, s2 = split2(x_ref[m] * sigma)
+        n1, n2 = split2(nu_ref[m])
+        left = jnp.concatenate([s1, s1, s2, s2], axis=0).astype(jnp.bfloat16)
+        right = jnp.concatenate([n1, n2, n1, n2], axis=0).astype(jnp.bfloat16)
         tastes = lax.dot_general(
             left, right, (((0,), (0,)), ((), ())), preferred_element_type=jnp.float32
         )
         return jnp.exp2(tastes)
+
+    chunks = [
+        slice(at, min(at + LANES, nu_ref.shape[2])) for at in range(0, nu_ref.shape[2], LANES)
+    ]
+
+    def denominators(weight, m, i, known):
+        for chunk in chunks:
+            e = held[m, :, chunk] if known is None else known[:, chunk]
+            inverse_ref[i : i + 1, chunk] = 1.0 + jnp.sum(weight * e, axis=0, keepdims=True)
 
     def sweep(weights, first):
         def body(g, total):
             base = g * group
+            if first:
+                nu_load(g).wait()
             local = pltpu.roll(weights, lax.rem(LANES - base, LANES), 1)
+            for i in range(group):
+                known = None
+                if first:
+                    known = raised_tastes(base + i)
+                    held[base + i] = known
+                denominators(local[:, i : i + 1], base + i, i, known)
+            inverse_ref[0:group] = 1.0 / inverse_ref[0:group]
             part = jnp.zeros((slots, LANES), jnp.float32)
             for i in range(group):
-                if first:
-                    e = raised_tastes(base + i)
-                    held[base + i] = e
-                else:
-                    e = held[base + i]
-                denominator = 1.0 + jnp.sum(local[:, i : i + 1] * e, axis=0, keepdims=True)
-                column = jnp.sum(e * (1.0 / denominator), axis=1, keepdims=True)
-                part = jnp.where(lane == i, column, part)
+                column = None
+                for chunk in chunks:
+                    term = held[base + i, :, chunk] * inverse_ref[i : i + 1, chunk]
+                    column = term if column is None else column + term
+                part = jnp.where(lane == i, jnp.sum(column, axis=1, keepdims=True), part)
             return total + pltpu.roll(part, base, 1)
 
         return lax.fori_loop(0, markets // group, body, jnp.zeros((slots, LANES), jnp.float32))
+
+    def fold(value):
+        if folds == slots:
+            return value
+        low = jnp.concatenate(
+            [value[folds:], jnp.zeros((2 * folds - slots, LANES), jnp.float32)], axis=0
+        )
+        return value[0:folds] + pltpu.roll(low, LANES // 2, 1)
+
+    def unfold(value):
+        if folds == slots:
+            return value
+        return jnp.concatenate(
+            [value, pltpu.roll(value, LANES // 2, 1)[0 : slots - folds]], axis=0
+        )
 
     def part_copy(it, k):
         return pltpu.make_async_remote_copy(
@@ -139,10 +204,11 @@
             device_id_type=MESH,
         )
 
+    norms = []
     for it in range(ITERS):
         weights = jnp.where(usable, jnp.exp(mean), 0.0)
         partial_value = sweep(weights, it == 0)
-        part_slots[it, my_draw] = partial_value
+        part_slots[it, my_draw] = fold(partial_value)
         if it == 0:
             pl.semaphore_wait(barrier, draws - 1 + chips - 1)
         for k in range(1, draws):
@@ -152,11 +218,11 @@
         total = part_slots[it, 0]
         for d in range(1, draws):
             total = total + part_slots[it, d]
-        shares = weights * total * inverse
+        shares = weights * unfold(total) * inverse
         change = jnp.where(usable, log_share - jnp.log(jnp.where(usable, shares, 1.0)), 0.0)
         peak = jnp.max(jnp.abs(change), axis=0, keepdims=True)
         peak = jnp.max(peak, axis=1, keepdims=True)
-        peak_slots[it, 0] = jnp.broadcast_to(peak, (8, LANES))
+        peak_slots[it, 0] = jnp.broadcast_to(peak, (1, LANES))
         for k in range(1, chips):
             peak_copy(it, k).start()
         for k in range(1, chips):
@@ -164,8 +230,7 @@
         largest = peak_slots[it, 0]
         for k in range(1, chips):
             largest = jnp.maximum(largest, peak_slots[it, k])
-        norms_out[it] = largest[0, 0]
-        largest = largest[0:1, :]
+        norms.append(largest)
         mean = mean + jnp.minimum(1.0, step_cap / (largest + epsilon)) * change
 
     weights = jnp.where(usable, jnp.exp(mean), 0.0)
@@ -173,6 +238,13 @@
     doubled = jnp.where(
         lax.broadcasted_iota(jnp.int32, (slots, slots + 8), 1) < slots, 2.0, 1.0
     )
+
+    cores = 2 if draws % 2 == 0 else 1
+
+    def partner(k):
+        chip = (my_draw // cores + (k - 1) // cores + 1) % (draws // cores)
+        core = (my_draw + k) % cores
+        return chip * cores + core
 
     def cross_copy(k):
         return pltpu.make_async_remote_copy(
@@ -180,16 +252,15 @@
             dst_ref=cross_slots.at[k - 1],
             send_sem=cross_send_sem.at[k - 1],
             recv_sem=cross_recv_sem.at[k - 1],
-            device_id={"draw": lax.rem(my_draw + k, draws)},
+            device_id={"draw": partner(k)},
             device_id_type=MESH,
         )
 
     def last_sweep(k, carry):
-        base = lax.rem(my_draw + k, draws) * own
+        base = partner(k) * own
         local = pltpu.roll(weights, lax.rem(LANES - base, LANES), 1)
         for i in range(own):
-            e = held[base + i]
-            raised = local[:, i : i + 1] * e
+            raised = local[:, i : i + 1] * held[base + i]
             denominator = 1.0 + jnp.sum(raised, axis=0, keepdims=True)
             chance = raised * (1.0 / denominator)
             both = jnp.concatenate([chance, chance - rounded(chance)], axis=0)
@@ -214,28 +285,30 @@
 
     square[0:slots, :] = mean
     mean_out[...] = square[...].T[0:markets, 0:slots]
+    for it in range(ITERS):
+        norms_out[it] = norms[it][0, 0]
 
     for k in range(1, draws):
         cross_copy(k).wait()
 
-    eye = (row == lane)[:, 0:slots]
+    eye = jnp.where(row == lane, 1.0, 0.0)
     for pair in range(cross_send.shape[1]):
         total = cross_send[draws - 1, pair]
         for k in range(1, draws):
             total = total + cross_slots[k - 1, pair]
+        square[0:slots, :] = total
+        turned = square[...].T
         for i in range(pack):
             if pair * pack + i >= own:
                 continue
             wide = total if i == 0 else pltpu.roll(total, LANES - i * half, 1)
-            square[0:slots, :] = wide
-            turned = square[...].T[0:slots, 0:slots]
-            cross = 0.5 * (wide[:, 0:slots] + turned)
+            cross = 0.5 * (wide[:, 0:slots] + turned[i * half : i * half + slots, 0:slots])
             count = counts_ref[my_draw * own + pair * pack + i]
             here = row < count
             divisor = jnp.where(here, wide, 1.0)[:, slots : slots + 1]
             jac_out[pair * pack + i] = jnp.where(
                 (here & (lane < count))[:, 0:slots],
-                jnp.where(eye, 1.0, 0.0) - cross / divisor,
+                eye[:, 0:slots] - cross / divisor,
                 0.0,
             )
 
@@ -246,6 +319,7 @@
     draws, chips = lax.axis_size("draw"), lax.axis_size("mkt")
     own = markets // draws
     half = LANES // 2 if slots + 8 <= LANES // 2 else LANES
+    folds = -(-slots // 16) * 8 if markets <= LANES // 2 else slots
     blocks = -(-own // (LANES // half))
     vmem = pl.BlockSpec(memory_space=pltpu.VMEM)
     smem = pl.BlockSpec(memory_space=pltpu.SMEM)
@@ -257,13 +331,20 @@
             jax.ShapeDtypeStruct((own, slots, slots), f32),
             jax.ShapeDtypeStruct((ITERS,), f32),
         ),
-        in_specs=[smem, smem, vmem, vmem, vmem, vmem],
+        in_specs=[pl.BlockSpec(memory_space=pltpu.HBM)] * 6,
         out_specs=(vmem, vmem, smem),
         scratch_shapes=[
+            pltpu.SMEM((coefs,), f32),
+            pltpu.SMEM((markets,), jnp.int32),
+            pltpu.VMEM((1, markets), jnp.int32),
+            pltpu.VMEM((markets, slots), f32),
+            pltpu.VMEM((markets, coefs, slots), f32),
+            pltpu.VMEM((markets, coefs, consumers), f32),
             pltpu.VMEM((markets, slots, consumers), f32),
+            pltpu.VMEM((divisor_up_to(markets, GROUP), consumers), f32),
             pltpu.VMEM((LANES, LANES), f32),
-            pltpu.VMEM((ITERS, draws, slots, LANES), f32),
-            pltpu.VMEM((ITERS, chips, 8, LANES), f32),
+            pltpu.VMEM((ITERS, draws, folds, LANES), f32),
+            pltpu.VMEM((ITERS, chips, 1, LANES), f32),
             pltpu.VMEM((draws, blocks, slots, LANES), f32),
             pltpu.VMEM((draws, blocks, slots, LANES), f32),
             pltpu.SemaphoreType.DMA((ITERS, draws)),
@@ -272,9 +353,11 @@
             pltpu.SemaphoreType.DMA((ITERS, chips)),
             pltpu.SemaphoreType.DMA((draws,)),
             pltpu.SemaphoreType.DMA((draws,)),
+            pltpu.SemaphoreType.DMA((5,)),
+            pltpu.SemaphoreType.DMA((markets // divisor_up_to(markets, GROUP),)),
         ],
         compiler_params=pltpu.CompilerParams(
-            collective_id=0, has_side_effects=True, vmem_limit_bytes=48 * 1024 * 1024
+            collective_id=0, has_side_effects=True, vmem_limit_bytes=VMEM_LIMIT
         ),
         name="contraction",
     )(

time: 53.7 us -> 47.6 us (0.89)
  Pallas kernels: 47.2 us -> 43.2 us
  local copies, waits for them, and re-layouts: 5.3 us -> 3.59 us
    pallas_call x1, Pallas kernels: 47.2 us -> 43.2 us  [shards(): pl.pallas_call(functools.partial(kernel, draws, chips, 1.0 / (consumers *...]
    unnamed x13 -> x5, local copies, waits for them, and re-layouts: 5.3 us -> 3.59 us
where the time goes in v2:
time: 47.6 us; the launch traced here: 47.4 us
  Pallas kernels  43.2 us (91%)
  local copies, waits for them, and re-layouts  3.59 us (8%)
  between operations  0.64 us (1%)
    pallas_call x1, Pallas kernels, shards(): pl.pallas_call(functools.partial(kernel, draws, chips, 1.0 / (consumers *...  43.2 us
    unnamed x5, local copies, waits for them, and re-layouts  3.59 us

profile of v2, /device:TPU:0, one launch (start us, length us, event | category | flops | bytes accessed | tf_op | source)
XLA Modules:
  0.0 47.4 jit_solution(83282647750669440)
XLA Ops:
  0.6 43.2 %contraction.1 = (f32[48,56]{1,0:T(8,128)}, f32[12,56,56]{2,1,0:T(8,128)}, f32[3]{0:T(128)}) custom-call(f32[8]{0:T(128)} %sigma_hbm.1, s32[48]{0:T(128)} %counts_hbm.1, s32[1,48]{1,0:T(1,128)} %bitcast.3, f32[48,56]{1,0:T(8,128)} %log_share_hbm.1, f32[48,8,56]{2,1,0:T(8,128)} %bitcast.2, f32[48,8,512]{2,1,0:T(8,128)} %nu_hbm.1), custom_call_target="tpu_custom_call" | custom-call | tf_op jit(solution)/shard_map/contraction/pallas_call | solution.py:327
  43.8 1.3 %copy.11 = f32[48,56]{1,0:T(8,128)} copy(f32[48,56]{1,0:T(8,128)} %get-tuple-element.6) | data formatting | bytes 21504
  45.2 0.0 copy-start
  45.2 1.7 %copy.12 = f32[12,56,56]{2,1,0:T(8,128)} copy(f32[12,56,56]{2,1,0:T(8,128)} %get-tuple-element.7) | data formatting | bytes 301056
  46.9 0.0 copy-done
  46.9 0.5 %copy.13 = f32[3]{0:T(128)} copy(f32[3]{0:T(128)S(1)} %copy-done) | data formatting | bytes 24
Async XLA Ops:
  45.2 1.7 %copy-start = (f32[3]{0:T(128)S(1)}, f32[3]{0:T(128)}, u32[]{:S(2)}) copy-start(f32[3]{0:T(128)} %get-tuple-element.8) | copy-start | bytes 40

commit v3 on v2

--- a/solution.py
+++ b/solution.py
@@ -52,6 +52,8 @@
     nu_ref,
     held,
     inverse_ref,
+    weights_ref,
+    turned_ref,
     square,
     part_slots,
     peak_slots,
@@ -68,10 +70,10 @@
 ):
     markets, coefs, slots = x_ref.shape
     own = markets // draws
-    half = LANES // 2 if slots + 8 <= LANES // 2 else LANES
-    pack = LANES // half
-    group = divisor_up_to(markets, GROUP)
-    folds = part_slots.shape[2]
+    half = LANES // 2
+    tiles = slots // 8
+    group = divisor_up_to(markets, min(GROUP, LANES // tiles))
+    groups = markets // group
     my_draw = lax.axis_index("draw")
     my_mkt = lax.axis_index("mkt")
 
@@ -94,7 +96,7 @@
 
     for load in loads:
         load.start()
-    for g in range(markets // group):
+    for g in range(groups):
         nu_load(g).start()
 
     barrier = pltpu.get_barrier_semaphore()
@@ -140,59 +142,101 @@
         slice(at, min(at + LANES, nu_ref.shape[2])) for at in range(0, nu_ref.shape[2], LANES)
     ]
 
-    def denominators(weight, m, i, known):
-        for chunk in chunks:
-            e = held[m, :, chunk] if known is None else known[:, chunk]
-            inverse_ref[i : i + 1, chunk] = 1.0 + jnp.sum(weight * e, axis=0, keepdims=True)
-
-    def sweep(weights, first):
-        def body(g, total):
+    lane8 = lax.broadcasted_iota(jnp.int32, (8, LANES), 1)
+    row8 = lax.broadcasted_iota(jnp.int32, (8, LANES), 0)
+
+    def within(tile):
+        return (lane8 >= tile * group) & (lane8 < (tile + 1) * group)
+
+    def packed(value, g):
+        total = jnp.zeros((8, LANES), jnp.float32)
+        for t in range(tiles):
+            shift = ((t - g) * group) % LANES
+            moved = value[8 * t : 8 * t + 8]
+            moved = pltpu.roll(moved, shift, 1) if shift else moved
+            total = jnp.where(within(t), moved, total)
+        return total
+
+    def unpacked(values):
+        rows = []
+        for t in range(tiles):
+            total = jnp.zeros((8, LANES), jnp.float32)
+            for g in range(groups):
+                shift = ((g - t) * group) % LANES
+                moved = pltpu.roll(values[g], shift, 1) if shift else values[g]
+                total = jnp.where(within(g), moved, total)
+            rows.append(total)
+        return jnp.concatenate(rows, axis=0)
+
+    product = row8
+    for t in range(1, tiles):
+        product = jnp.where(lane8 >= t * group, row8 + 8 * t, product)
+    ls = [packed(log_share, g) for g in range(groups)]
+    means = [packed(mean, g) for g in range(groups)]
+    wide_counts = jnp.broadcast_to(counts, (slots, LANES))
+    valid = [
+        (product.astype(jnp.float32) < packed(wide_counts, g)) & (lane8 < tiles * group)
+        for g in range(groups)
+    ]
+
+    chunks = [
+        slice(at, min(at + LANES, nu_ref.shape[2])) for at in range(0, nu_ref.shape[2], LANES)
+    ]
+
+    def weight_column(local, i):
+        return jnp.concatenate(
+            [local[:, t * group + i : t * group + i + 1] for t in range(tiles)], axis=0
+        )
+
+    def part_copy(it, k, g):
+        return pltpu.make_async_remote_copy(
+            src_ref=part_slots.at[it, my_draw, g],
+            dst_ref=part_slots.at[it, my_draw, g],
+            send_sem=part_send_sem.at[it, k - 1, g],
+            recv_sem=part_recv_sem.at[it, k - 1, g],
+            device_id={"draw": lax.rem(my_draw + k, draws)},
+            device_id_type=MESH,
+        )
+
+    def sweep(it):
+        def body(g, carry):
             base = g * group
-            if first:
+            if it == 0:
                 nu_load(g).wait()
-            local = pltpu.roll(weights, lax.rem(LANES - base, LANES), 1)
+            local = weights_ref[g]
             for i in range(group):
+                weight = weight_column(local, i)
                 known = None
-                if first:
+                if it == 0:
                     known = raised_tastes(base + i)
                     held[base + i] = known
-                denominators(local[:, i : i + 1], base + i, i, known)
-            inverse_ref[0:group] = 1.0 / inverse_ref[0:group]
-            part = jnp.zeros((slots, LANES), jnp.float32)
+                for chunk in chunks:
+                    e = held[base + i, :, chunk] if known is None else known[:, chunk]
+                    inverse_ref[i : i + 1, chunk] = 1.0 + jnp.sum(
+                        weight * e, axis=0, keepdims=True
+                    )
+            inverse_ref[...] = 1.0 / inverse_ref[...]
+            part = jnp.zeros((8, LANES), jnp.float32)
             for i in range(group):
                 column = None
                 for chunk in chunks:
                     term = held[base + i, :, chunk] * inverse_ref[i : i + 1, chunk]
                     column = term if column is None else column + term
-                part = jnp.where(lane == i, jnp.sum(column, axis=1, keepdims=True), part)
-            return total + pltpu.roll(part, base, 1)
-
-        return lax.fori_loop(0, markets // group, body, jnp.zeros((slots, LANES), jnp.float32))
-
-    def fold(value):
-        if folds == slots:
-            return value
-        low = jnp.concatenate(
-            [value[folds:], jnp.zeros((2 * folds - slots, LANES), jnp.float32)], axis=0
-        )
-        return value[0:folds] + pltpu.roll(low, LANES // 2, 1)
-
-    def unfold(value):
-        if folds == slots:
-            return value
-        return jnp.concatenate(
-            [value, pltpu.roll(value, LANES // 2, 1)[0 : slots - folds]], axis=0
-        )
-
-    def part_copy(it, k):
-        return pltpu.make_async_remote_copy(
-            src_ref=part_slots.at[it, my_draw],
-            dst_ref=part_slots.at[it, my_draw],
-            send_sem=part_send_sem.at[it, k - 1],
-            recv_sem=part_recv_sem.at[it, k - 1],
-            device_id={"draw": lax.rem(my_draw + k, draws)},
-            device_id_type=MESH,
-        )
+                column = jnp.sum(column, axis=1, keepdims=True)
+                for t in range(tiles):
+                    part = jnp.where(lane8 == t * group + i, column[8 * t : 8 * t + 8], part)
+            part_slots[it, my_draw, g] = part
+            if it == 0:
+
+                @pl.when(g == 0)
+                def _():
+                    pl.semaphore_wait(barrier, draws - 1 + chips - 1)
+
+            for k in range(1, draws):
+                part_copy(it, k, g).start()
+            return carry
+
+        lax.fori_loop(0, groups, body, 0)
 
     def peak_copy(it, k):
         return pltpu.make_async_remote_copy(
@@ -206,21 +250,23 @@
 
     norms = []
     for it in range(ITERS):
-        weights = jnp.where(usable, jnp.exp(mean), 0.0)
-        partial_value = sweep(weights, it == 0)
-        part_slots[it, my_draw] = fold(partial_value)
-        if it == 0:
-            pl.semaphore_wait(barrier, draws - 1 + chips - 1)
-        for k in range(1, draws):
-            part_copy(it, k).start()
-        for k in range(1, draws):
-            part_copy(it, k).wait()
-        total = part_slots[it, 0]
-        for d in range(1, draws):
-            total = total + part_slots[it, d]
-        shares = weights * unfold(total) * inverse
-        change = jnp.where(usable, log_share - jnp.log(jnp.where(usable, shares, 1.0)), 0.0)
-        peak = jnp.max(jnp.abs(change), axis=0, keepdims=True)
+        weights = [jnp.where(valid[g], jnp.exp(means[g]), 0.0) for g in range(groups)]
+        for g in range(groups):
+            weights_ref[g] = weights[g]
+        sweep(it)
+        changes = []
+        peak = jnp.zeros((8, LANES), jnp.float32)
+        for g in range(groups):
+            for k in range(1, draws):
+                part_copy(it, k, g).wait()
+            total = part_slots[it, 0, g]
+            for d in range(1, draws):
+                total = total + part_slots[it, d, g]
+            shares = jnp.where(valid[g], weights[g] * total * inverse, 1.0)
+            change = jnp.where(valid[g], ls[g] - jnp.log(shares), 0.0)
+            changes.append(change)
+            peak = jnp.maximum(peak, jnp.abs(change))
+        peak = jnp.max(peak, axis=0, keepdims=True)
         peak = jnp.max(peak, axis=1, keepdims=True)
         peak_slots[it, 0] = jnp.broadcast_to(peak, (1, LANES))
         for k in range(1, chips):
@@ -231,14 +277,12 @@
         for k in range(1, chips):
             largest = jnp.maximum(largest, peak_slots[it, k])
         norms.append(largest)
-        mean = mean + jnp.minimum(1.0, step_cap / (largest + epsilon)) * change
-
+        step = jnp.minimum(1.0, step_cap / (largest + epsilon))
+        means = [means[g] + step * changes[g] for g in range(groups)]
+
+    mean = unpacked(means)
     weights = jnp.where(usable, jnp.exp(mean), 0.0)
     ones = jnp.ones((8, nu_ref.shape[2]), jnp.float32)
-    doubled = jnp.where(
-        lax.broadcasted_iota(jnp.int32, (slots, slots + 8), 1) < slots, 2.0, 1.0
-    )
-
     cores = 2 if draws % 2 == 0 else 1
 
     def partner(k):
@@ -259,21 +303,41 @@
     def last_sweep(k, carry):
         base = partner(k) * own
         local = pltpu.roll(weights, lax.rem(LANES - base, LANES), 1)
-        for i in range(own):
+        def market(i):
             raised = local[:, i : i + 1] * held[base + i]
             denominator = 1.0 + jnp.sum(raised, axis=0, keepdims=True)
             chance = raised * (1.0 / denominator)
-            both = jnp.concatenate([chance, chance - rounded(chance)], axis=0)
-            right = jnp.concatenate([chance, ones], axis=0).astype(jnp.bfloat16)
+            low = chance - rounded(chance)
+            left = jnp.concatenate([chance, low], axis=0).astype(jnp.bfloat16)
+            right = jnp.concatenate([chance, ones, low], axis=0).astype(jnp.bfloat16)
             products = lax.dot_general(
-                both.astype(jnp.bfloat16),
-                right,
-                (((1,), (1,)), ((), ())),
-                preferred_element_type=jnp.float32,
+                left, right, (((1,), (1,)), ((), ())), preferred_element_type=jnp.float32
             )
-            merged = products[0:slots] + products[slots:] * doubled
-            at = (i % pack) * half
-            cross_send[k - 1, i // pack, :, at : at + slots + 8] = merged
+            products = jnp.concatenate(
+                [products, jnp.zeros((2 * slots, LANES - 2 * slots - 8), jnp.float32)], axis=1
+            )
+            high = products[0:slots]
+            return high + products[slots:] + jnp.where(
+                lane < slots, pltpu.roll(high, LANES - slots - 8, 1), 0.0
+            )
+
+        def pair_block(first):
+            low = market(first)
+            if first + 1 < own:
+                high = pltpu.roll(market(first + 1), 1, 1)
+            else:
+                high = low
+            return jnp.where(
+                lane <= row, low, jnp.where(lane == slots + 2, pltpu.roll(low, 2, 1), high)
+            )
+
+        for block in range(cross_send.shape[1]):
+            value = pair_block(4 * block)
+            if 4 * block + 2 < own:
+                value = jnp.where(
+                    lane < half, value, pltpu.roll(pair_block(4 * block + 2), half, 1)
+                )
+            cross_send[k - 1, block] = value
 
         @pl.when(k < draws)
         def _():
@@ -292,25 +356,32 @@
         cross_copy(k).wait()
 
     eye = jnp.where(row == lane, 1.0, 0.0)
-    for pair in range(cross_send.shape[1]):
-        total = cross_send[draws - 1, pair]
+    for block in range(cross_send.shape[1]):
+        total = cross_send[draws - 1, block]
         for k in range(1, draws):
-            total = total + cross_slots[k - 1, pair]
+            total = total + cross_slots[k - 1, block]
         square[0:slots, :] = total
-        turned = square[...].T
-        for i in range(pack):
-            if pair * pack + i >= own:
+        turned_ref[...] = square[...].T
+        for i in range(4):
+            m = 4 * block + i
+            if m >= own:
                 continue
-            wide = total if i == 0 else pltpu.roll(total, LANES - i * half, 1)
-            cross = 0.5 * (wide[:, 0:slots] + turned[i * half : i * half + slots, 0:slots])
-            count = counts_ref[my_draw * own + pair * pack + i]
+            at = (i // 2) * half
+            wide = pltpu.roll(total, LANES - at, 1) if at else total
+            if i % 2 == 0:
+                cross = jnp.where(lane <= row, wide, turned_ref[at : at + slots, :])
+                share = wide[:, slots + 2 : slots + 3]
+            else:
+                cross = jnp.where(
+                    lane >= row,
+                    pltpu.roll(wide, LANES - 1, 1),
+                    turned_ref[at + 1 : at + 1 + slots, :],
+                )
+                share = wide[:, slots + 1 : slots + 2]
+            count = counts_ref[my_draw * own + m]
             here = row < count
-            divisor = jnp.where(here, wide, 1.0)[:, slots : slots + 1]
-            jac_out[pair * pack + i] = jnp.where(
-                (here & (lane < count))[:, 0:slots],
-                eye[:, 0:slots] - cross / divisor,
-                0.0,
-            )
+            divisor = jnp.where(here[:, 0:1], share, 1.0)
+            jac_out[m] = jnp.where(here & (lane < count), eye - cross / divisor, 0.0)[:, 0:slots]
 
 
 def shards(x_char, nu_draws, coef_sigma, log_share, counts):
@@ -318,9 +389,9 @@
     consumers = nu_draws.shape[2]
     draws, chips = lax.axis_size("draw"), lax.axis_size("mkt")
     own = markets // draws
-    half = LANES // 2 if slots + 8 <= LANES // 2 else LANES
-    folds = -(-slots // 16) * 8 if markets <= LANES // 2 else slots
-    blocks = -(-own // (LANES // half))
+    blocks = -(-own // 4)
+    group = divisor_up_to(markets, min(GROUP, LANES // (slots // 8)))
+    groups = markets // group
     vmem = pl.BlockSpec(memory_space=pltpu.VMEM)
     smem = pl.BlockSpec(memory_space=pltpu.SMEM)
     f32 = jnp.float32
@@ -341,20 +412,22 @@
             pltpu.VMEM((markets, coefs, slots), f32),
             pltpu.VMEM((markets, coefs, consumers), f32),
             pltpu.VMEM((markets, slots, consumers), f32),
-            pltpu.VMEM((divisor_up_to(markets, GROUP), consumers), f32),
+            pltpu.VMEM((group, consumers), f32),
+            pltpu.VMEM((groups, 8, LANES), f32),
             pltpu.VMEM((LANES, LANES), f32),
-            pltpu.VMEM((ITERS, draws, folds, LANES), f32),
+            pltpu.VMEM((LANES, LANES), f32),
+            pltpu.VMEM((ITERS, draws, groups, 8, LANES), f32),
             pltpu.VMEM((ITERS, chips, 1, LANES), f32),
             pltpu.VMEM((draws, blocks, slots, LANES), f32),
             pltpu.VMEM((draws, blocks, slots, LANES), f32),
-            pltpu.SemaphoreType.DMA((ITERS, draws)),
-            pltpu.SemaphoreType.DMA((ITERS, draws)),
+            pltpu.SemaphoreType.DMA((ITERS, draws, groups)),
+            pltpu.SemaphoreType.DMA((ITERS, draws, groups)),
             pltpu.SemaphoreType.DMA((ITERS, chips)),
             pltpu.SemaphoreType.DMA((ITERS, chips)),
             pltpu.SemaphoreType.DMA((draws,)),
             pltpu.SemaphoreType.DMA((draws,)),
             pltpu.SemaphoreType.DMA((5,)),
-            pltpu.SemaphoreType.DMA((markets // divisor_up_to(markets, GROUP),)),
+            pltpu.SemaphoreType.DMA((groups,)),
         ],
         compiler_params=pltpu.CompilerParams(
             collective_id=0, has_side_effects=True, vmem_limit_bytes=VMEM_LIMIT

time: 47.6 us -> 43.4 us (0.912)
  Pallas kernels: 43.2 us -> 39 us
    pallas_call x1, Pallas kernels: 43.2 us -> 39 us  [shards(): pl.pallas_call(functools.partial(kernel, draws, chips, 1.0 / (consumers *...]
where the time goes in v3:
time: 43.4 us; the launch traced here: 43.2 us
  Pallas kernels  39 us (90%)
  local copies, waits for them, and re-layouts  3.59 us (8%)
  between operations  0.64 us (1%)
    pallas_call x1, Pallas kernels, shards(): pl.pallas_call(functools.partial(kernel, draws, chips, 1.0 / (consumers *...  39 us
    unnamed x5, local copies, waits for them, and re-layouts  3.59 us

profile of v3, /device:TPU:0, one launch (start us, length us, event | category | flops | bytes accessed | tf_op | source)
XLA Modules:
  0.0 43.2 jit_solution(13500990839506811416)
XLA Ops:
  0.6 39.0 %contraction.1 = (f32[48,56]{1,0:T(8,128)}, f32[12,56,56]{2,1,0:T(8,128)}, f32[3]{0:T(128)}) custom-call(f32[8]{0:T(128)} %sigma_hbm.1, s32[48]{0:T(128)} %counts_hbm.1, s32[1,48]{1,0:T(1,128)} %bitcast.3, f32[48,56]{1,0:T(8,128)} %log_share_hbm.1, f32[48,8,56]{2,1,0:T(8,128)} %bitcast.2, f32[48,8,512]{2,1,0:T(8,128)} %nu_hbm.1), custom_call_target="tpu_custom_call" | custom-call | tf_op jit(solution)/shard_map/contraction/pallas_call | solution.py:398
  39.6 1.3 %copy.11 = f32[48,56]{1,0:T(8,128)} copy(f32[48,56]{1,0:T(8,128)} %get-tuple-element.6) | data formatting | bytes 21504
  41.0 0.0 copy-start
  41.0 1.7 %copy.12 = f32[12,56,56]{2,1,0:T(8,128)} copy(f32[12,56,56]{2,1,0:T(8,128)} %get-tuple-element.7) | data formatting | bytes 301056
  42.7 0.0 copy-done
  42.7 0.5 %copy.13 = f32[3]{0:T(128)} copy(f32[3]{0:T(128)S(1)} %copy-done) | data formatting | bytes 24
Async XLA Ops:
  41.0 1.7 %copy-start = (f32[3]{0:T(128)S(1)}, f32[3]{0:T(128)}, u32[]{:S(2)}) copy-start(f32[3]{0:T(128)} %get-tuple-element.8) | copy-start | bytes 40

commit v4 on v3

--- a/solution.py
+++ b/solution.py
@@ -11,7 +11,7 @@
 ITERS = 3
 LANES = 128
 GROUP = 16
-VMEM_LIMIT = 66_500_000
+VMEM_LIMIT = 48 * 1024 * 1024
 MESH = pl.DeviceIdType.MESH
 
 step_cap = 0.25
@@ -381,7 +381,7 @@
             count = counts_ref[my_draw * own + m]
             here = row < count
             divisor = jnp.where(here[:, 0:1], share, 1.0)
-            jac_out[m] = jnp.where(here & (lane < count), eye - cross / divisor, 0.0)[:, 0:slots]
+            jac_out[m] = jnp.where(here & (lane < count), eye - cross * (1.0 / divisor), 0.0)[:, 0:slots]
 
 
 def shards(x_char, nu_draws, coef_sigma, log_share, counts):
@@ -434,12 +434,17 @@
         ),
         name="contraction",
     )(
-        coef_sigma,
-        counts,
-        counts[None, :],
-        log_share,
-        jnp.swapaxes(x_char, 1, 2),
-        nu_draws,
+        *(
+            pltpu.with_memory_space_constraint(operand, pltpu.HBM)
+            for operand in (
+                coef_sigma,
+                counts,
+                counts[None, :],
+                log_share,
+                jnp.swapaxes(x_char, 1, 2),
+                nu_draws,
+            )
+        )
     )
 
 

time: 43.4 us -> 41.4 us (0.954)
  local copies, waits for them, and re-layouts: 3.59 us -> 1.85 us
    unnamed x5 -> x3, local copies, waits for them, and re-layouts: 3.59 us -> 1.85 us
where the time goes in v4:
time: 41.4 us; the launch traced here: 41.2 us
  Pallas kernels  38.7 us (93%)
  local copies, waits for them, and re-layouts  1.85 us (4%)
  between operations  0.64 us (2%)
    pallas_call x1, Pallas kernels, shards(): pl.pallas_call(functools.partial(kernel, draws, chips, 1.0 / (consumers *...  38.7 us
    unnamed x3, local copies, waits for them, and re-layouts  1.85 us

profile of v4, /device:TPU:0, one launch (start us, length us, event | category | flops | bytes accessed | tf_op | source)
XLA Modules:
  0.0 41.2 jit_solution(1427230268113411160)
XLA Ops:
  0.6 38.7 %contraction.1 = (f32[48,56]{1,0:T(8,128)S(1)}, f32[12,56,56]{2,1,0:T(8,128)S(1)}, f32[3]{0:T(128)S(1)}) custom-call(f32[8]{0:T(128)} %sigma_hbm.1, s32[48]{0:T(128)} %counts_hbm.1, s32[1,48]{1,0:T(1,128)} %bitcast.3, f32[48,56]{1,0:T(8,128)} %log_share_hbm.1, f32[48,8,56]{2,1,0:T(8,128)} %bitcast.2, f32[48,8,512]{2,1,0:T(8,128)} %nu_hbm.1), custom_call_target="tpu_custom_call" | custom-call | tf_op jit(solution)/shard_map/contraction/pallas_call | solution.py:398
  39.4 0.6 %copy.11 = f32[48,56]{1,0:T(8,128)} copy(f32[48,56]{1,0:T(8,128)S(1)} %get-tuple-element.6) | data formatting | bytes 21504
  40.0 0.7 %copy.12 = f32[12,56,56]{2,1,0:T(8,128)} copy(f32[12,56,56]{2,1,0:T(8,128)S(1)} %get-tuple-element.7) | data formatting | bytes 301056
  40.7 0.5 %copy.13 = f32[3]{0:T(128)} copy(f32[3]{0:T(128)S(1)} %get-tuple-element.8) | data formatting | bytes 24

commit v5 on v4

--- a/solution.py
+++ b/solution.py
@@ -258,7 +258,7 @@
         peak = jnp.zeros((8, LANES), jnp.float32)
         for g in range(groups):
             for k in range(1, draws):
-                part_copy(it, k, g).wait()
+                part_copy(it, k, g).wait_recv()
             total = part_slots[it, 0, g]
             for d in range(1, draws):
                 total = total + part_slots[it, d, g]
@@ -269,10 +269,10 @@
         peak = jnp.max(peak, axis=0, keepdims=True)
         peak = jnp.max(peak, axis=1, keepdims=True)
         peak_slots[it, 0] = jnp.broadcast_to(peak, (1, LANES))
-        for k in range(1, chips):
+        for k in sorted(range(1, chips), key=lambda k: -min(k, chips - k)):
             peak_copy(it, k).start()
         for k in range(1, chips):
-            peak_copy(it, k).wait()
+            peak_copy(it, k).wait_recv()
         largest = peak_slots[it, 0]
         for k in range(1, chips):
             largest = jnp.maximum(largest, peak_slots[it, k])
@@ -352,6 +352,12 @@
     for it in range(ITERS):
         norms_out[it] = norms[it][0, 0]
 
+    for it in range(ITERS):
+        for k in range(1, chips):
+            peak_copy(it, k).wait_send()
+        for k in range(1, draws):
+            for g in range(groups):
+                part_copy(it, k, g).wait_send()
     for k in range(1, draws):
         cross_copy(k).wait()
 

time: 41.4 us -> 41.4 us (level)
  no operation moved by 1% of the time
where the time goes in v5:
time: 41.4 us; the launch traced here: 41.2 us
  Pallas kernels  38.7 us (93%)
  local copies, waits for them, and re-layouts  1.85 us (4%)
  between operations  0.64 us (2%)
    pallas_call x1, Pallas kernels, shards(): pl.pallas_call(functools.partial(kernel, draws, chips, 1.0 / (consumers *...  38.7 us
    unnamed x3, local copies, waits for them, and re-layouts  1.85 us

profile of v5, /device:TPU:0, one launch (start us, length us, event | category | flops | bytes accessed | tf_op | source)
XLA Modules:
  0.0 41.2 jit_solution(3586098109638927402)
XLA Ops:
  0.6 38.7 %contraction.1 = (f32[48,56]{1,0:T(8,128)S(1)}, f32[12,56,56]{2,1,0:T(8,128)S(1)}, f32[3]{0:T(128)S(1)}) custom-call(f32[8]{0:T(128)} %sigma_hbm.1, s32[48]{0:T(128)} %counts_hbm.1, s32[1,48]{1,0:T(1,128)} %bitcast.3, f32[48,56]{1,0:T(8,128)} %log_share_hbm.1, f32[48,8,56]{2,1,0:T(8,128)} %bitcast.2, f32[48,8,512]{2,1,0:T(8,128)} %nu_hbm.1), custom_call_target="tpu_custom_call" | custom-call | tf_op jit(solution)/shard_map/contraction/pallas_call | solution.py:404
  39.4 0.6 %copy.11 = f32[48,56]{1,0:T(8,128)} copy(f32[48,56]{1,0:T(8,128)S(1)} %get-tuple-element.6) | data formatting | bytes 21504
  40.0 0.7 %copy.12 = f32[12,56,56]{2,1,0:T(8,128)} copy(f32[12,56,56]{2,1,0:T(8,128)S(1)} %get-tuple-element.7) | data formatting | bytes 301056
  40.7 0.5 %copy.13 = f32[3]{0:T(128)} copy(f32[3]{0:T(128)S(1)} %get-tuple-element.8) | data formatting | bytes 24
